TPU v7x, 32 devices: a whole 2x2x4 slice. The times are simulated.
32 devices in a mesh: gx: 8 (over z, core), gy: 4 (over y, x).
Axes of the slice: x: 2, y: 2, z: 4, core: 2. Of those that a mesh axis runs over, the one named last changes fastest.
Arguments:
- init_re: float32 [1, 256, 4096], P(None, 'gx', 'gy'), may hold values from -6 to 6
- init_im: float32 [1, 256, 4096], P(None, 'gx', 'gy'), may hold values from -6 to 6
- onsite: float32 [256, 4096], P('gx', 'gy'), may hold values from -0.9 to 0.9
- bond_x: int32 [256, 4096], P('gx', 'gy'), may hold values from 0 to 15
- bond_y: int32 [256, 4096], P('gx', 'gy'), may hold values from 0 to 15
- hop_table: float32 [16], replicated, may hold values from 1.4 to 1.6
- centre: int32 [1, 2], replicated, may hold values from 0 to 255
- duration: float32 [1], replicated, may hold values from 0.55 to 0.6
Outputs:
- out_re: float32 [1, 256, 4096], P(None, 'gx', 'gy')
- out_im: float32 [1, 256, 4096], P(None, 'gx', 'gy')
- term_norms: float32 [2, 8, 1], replicated
All inputs are finite; a program needn't handle non-finite values.
Results may differ from a plain program's by a relative error of at most 0.0003.
Values sent between devices are 32-bit elements; how exact they have to be, the bound alone decides.
A program may use at most 64 MiB of HBM per device.

v0:
```python
import math
import jax
import jax.numpy as jnp
from jax import lax
from jax.sharding import PartitionSpec as P

TERMS = 8
STEPS = 2
SPECTRAL = 7.5
epsilon = 1e-06


def padded(block, sides, width):
    for axis, dim in sides:
        count = lax.axis_size(axis)
        forward = [(i, i + 1) for i in range(count - 1)]
        forward.append((count - 1, 0))
        backward = [(target, source) for source, target in forward]
        low = lax.ppermute(
            lax.slice_in_dim(block, block.shape[dim] - width, None, axis=dim), axis, forward
        )
        high = lax.ppermute(lax.slice_in_dim(block, 0, width, axis=dim), axis, backward)
        block = jnp.concatenate([low, block, high], axis=dim)
    return block


def bessel_weights(duration):
    argument = duration[0] * SPECTRAL
    halved = argument * 0.5
    weights = []
    for degree in range(TERMS):
        series = halved**degree / math.factorial(degree)
        summed = series
        for counter in range(1, 24):
            series = series * -(halved * halved) / (counter * (counter + degree))
            summed = summed + series
        weights.append(summed if degree == 0 else 2.0 * summed)
    return weights


def rotated(degree, real_part, imag_part):
    quarter = degree % 4
    if quarter == 0:
        return (real_part, imag_part)
    if quarter == 1:
        return (imag_part, -real_part)
    if quarter == 2:
        return (-real_part, -imag_part)
    return (-imag_part, real_part)


def falloff(positions, centres, extent):
    distance = jnp.mod(positions[None, :] - centres[:, None], extent)
    distance = jnp.minimum(distance, extent - distance).astype(jnp.float32)
    return distance * distance * (4.5 / (extent * extent))


def shrink(tensor, margin):
    if margin == 0:
        return tensor
    return tensor[..., margin : tensor.shape[-2] - margin, margin : tensor.shape[-1] - margin]


def apply_wide(grid_field, coeffs):
    potential = coeffs[0]
    hop_rows = coeffs[1]
    hop_cols = coeffs[2]
    result = potential[1:-1, 1:-1] * grid_field[..., 1:-1, 1:-1]
    result = result - hop_rows[1:-1, 1:-1] * grid_field[..., 2:, 1:-1]
    result = result - hop_rows[:-2, 1:-1] * grid_field[..., :-2, 1:-1]
    result = result - hop_cols[1:-1, 1:-1] * grid_field[..., 1:-1, 2:]
    result = result - hop_cols[1:-1, :-2] * grid_field[..., 1:-1, :-2]
    return result * (1.0 / SPECTRAL)


def per_device(init_re, init_im, onsite, bond_x, bond_y, hop_table, centre, duration):
    packets, rows_local, cols_local = init_re.shape
    rows_total = rows_local * lax.axis_size("gx")
    cols_total = cols_local * lax.axis_size("gy")
    cell_count = rows_total * cols_total
    classes = hop_table.shape[0]
    selector = jnp.arange(classes, dtype=jnp.int32)[:, None, None]
    table_column = hop_table[:, None, None]
    hop_down = jnp.sum(jnp.where(bond_x[None] == selector, table_column, 0.0), axis=0)
    hop_right = jnp.sum(jnp.where(bond_y[None] == selector, table_column, 0.0), axis=0)
    weights = bessel_weights(duration)
    row_index = lax.axis_index("gx") * rows_local + lax.iota(jnp.int32, rows_local)
    col_index = lax.axis_index("gy") * cols_local + lax.iota(jnp.int32, cols_local)
    row_fall = falloff(row_index, centre[:, 0], rows_total)
    col_fall = falloff(col_index, centre[:, 1], cols_total)
    envelope = jnp.exp(-(row_fall[:, :, None] + col_fall[:, None, :]))
    packet_state = jnp.stack([init_re * envelope, init_im * envelope])
    reach = TERMS - 1
    coeffs = padded(jnp.stack([onsite, hop_down, hop_right]), (("gx", 1), ("gy", 2)), reach)
    norm_rows = []
    for repeat in range(STEPS):
        current = padded(packet_state, (("gx", 2), ("gy", 3)), reach)
        margin = reach
        previous = current
        previous_margin = reach
        chebyshev = [packet_state]
        for chebyshev_degree in range(1, TERMS):
            applied = apply_wide(current, shrink(coeffs, reach - margin))
            if chebyshev_degree == 1:
                following = applied
            else:
                following = 2.0 * applied - shrink(previous, previous_margin - margin + 1)
            previous, previous_margin = (current, margin)
            current = following
            margin = margin - 1
            chebyshev.append(shrink(following, margin))
        accumulate = weights[0] * packet_state
        for degree in range(1, TERMS):
            real_rot, imag_rot = rotated(degree, chebyshev[degree][0], chebyshev[degree][1])
            accumulate = accumulate + weights[degree] * jnp.stack([real_rot, imag_rot])
        term_local = jnp.stack([jnp.sum(vector * vector, axis=(0, 2, 3)) for vector in chebyshev])
        state_local = jnp.sum(accumulate * accumulate, axis=(0, 2, 3))
        term_total, state_total = lax.psum((term_local, state_local), ("gx", "gy"))
        norm_rows.append(term_total / cell_count)
        rescale = lax.rsqrt(state_total / cell_count + epsilon)
        packet_state = accumulate * rescale[None, :, None, None]
    return (packet_state[0], packet_state[1], jnp.stack(norm_rows))


def solution(mesh):
    return jax.shard_map(
        per_device,
        mesh=mesh,
        in_specs=(
            P(None, "gx", "gy"),
            P(None, "gx", "gy"),
            P("gx", "gy"),
            P("gx", "gy"),
            P("gx", "gy"),
            P(),
            P(),
            P(),
        ),
        out_specs=(P(None, "gx", "gy"), P(None, "gx", "gy"), P()),
        check_vma=False,
    )
```

profile of v0, /device:TPU:0, one launch (start us, length us, event | category | flops | bytes accessed | tf_op | source)
XLA Modules:
  0.0 153.5 jit_solution(4384548073286884623)
XLA Ops:
  0.7 1.3 fusion.128
  3.3 1.1 multiply_bitcast_fusion
  5.0 4.1 %collective-permute-start.5 = (f32[2,1,7,1024]{3,2,1,0:T(8,128)S(1)}, f32[2,1,7,1024]{3,2,1,0:T(8,128)S(1)}, u32[]{:S(2)}, u32[]{:S(2)}) collective-permute-start(f32[2,1,7,1024]{3,2,1,0:T(8,128)S(1)} %get-tuple-element.80), channel_id=1, source_target_pairs={{4,0},{8,4},{12,8},{16,12},{20,16},{24,20},{28,24},{0,28},{5,1},{9... | collective-permute-start | bytes 172040 | tf_op jit(solution)/shard_map/ppermute | solution.py:22
  9.7 3.5 %collective-permute-start.1 = (f32[3,7,1024]{2,1,0:T(8,128)S(1)}, f32[3,7,1024]{2,1,0:T(8,128)S(1)}, u32[]{:S(2)}, u32[]{:S(2)}) collective-permute-start(f32[3,7,1024]{2,1,0:T(8,128)S(1)} %get-tuple-element.52), channel_id=1, source_target_pairs={{4,0},{8,4},{12,8},{16,12},{20,16},{24,20},{28,24},{0,28},{5,1},{9... | collective-permute-start | bytes 258056 | tf_op jit(solution)/shard_map/ppermute | solution.py:22
  16.0 3.4 %collective-permute-start.3 = (f32[3,46,7]{2,1,0:T(8,128)S(1)}, f32[3,46,7]{2,1,0:T(8,128)S(1)}, u32[]{:S(2)}, u32[]{:S(2)}) collective-permute-start(f32[3,46,7]{2,1,0:T(8,128)S(1)} %get-tuple-element.39), channel_id=1, source_target_pairs={{1,0},{2,1},{3,2},{0,3},{5,4},{6,5},{7,6},{4,7},{9,8},{10,9},{11,1... | collective-permute-start | bytes 11600 | tf_op jit(solution)/shard_map/ppermute | solution.py:22
  19.4 2.9 %collective-permute-start.7 = (f32[2,1,46,7]{3,2,1,0:T(8,128)S(1)}, f32[2,1,46,7]{3,2,1,0:T(8,128)S(1)}, u32[]{:S(2)}, u32[]{:S(2)}) collective-permute-start(f32[2,1,46,7]{3,2,1,0:T(8,128)S(1)} %get-tuple-element.53), channel_id=1, source_target_pairs={{1,0},{2,1},{3,2},{0,3},{5,4},{6,5},{7,6},{4,7},{9,8},{10,9},{11,1... | collective-permute-start | bytes 7736 | tf_op jit(solution)/shard_map/ppermute | solution.py:22
  22.4 1.8 %collective-permute-done.7 = f32[2,1,46,7]{3,2,1,0:T(8,128)S(1)} collective-permute-done((f32[2,1,46,7]{3,2,1,0:T(8,128)S(1)}, f32[2,1,46,7]{3,2,1,0:T(8,128)S(1)}, u32[]{:S(2)}, u32[]{:S(2)}) %collective-permute-start.7) | collective-permute-done | bytes 2608 | tf_op jit(solution)/shard_map/ppermute | solution.py:22
  24.2 3.2 %collective-permute-done.6 = f32[2,1,46,7]{3,2,1,0:T(8,128)S(1)} collective-permute-done((f32[2,1,46,7]{3,2,1,0:T(8,128)S(1)}, f32[2,1,46,7]{3,2,1,0:T(8,128)S(1)}, u32[]{:S(2)}, u32[]{:S(2)}) %collective-permute-start.6) | collective-permute-done | bytes 2608 | tf_op jit(solution)/shard_map/ppermute | solution.py:19
  30.3 0.8 fusion.65
  38.8 1.1 multiply_reduce_fusion.5
  39.9 0.9 multiply_reduce_fusion.11
  40.8 37.0 %psum.28 = f32[1]{0:T(128)} all-reduce(f32[1]{0:T(128)} %bitcast.29), channel_id=1, replica_groups=mesh['gx'=8,'gy'=4] {'gx','gy'}, use_global_device_ids=true, to_apply=%region_3.4 | all-reduce | flops 1 | bytes 8 | tf_op jit(solution)/shard_map/psum | solution.py:118
  79.3 3.5 %collective-permute-start.9 = (f32[2,1,7,1024]{3,2,1,0:T(8,128)S(1)}, f32[2,1,7,1024]{3,2,1,0:T(8,128)S(1)}, u32[]{:S(2)}, u32[]{:S(2)}) collective-permute-start(f32[2,1,7,1024]{3,2,1,0:T(8,128)S(1)} %get-tuple-element.76), channel_id=1, source_target_pairs={{4,0},{8,4},{12,8},{16,12},{20,16},{24,20},{28,24},{0,28},{5,1},{9... | collective-permute-start | bytes 172040 | tf_op jit(solution)/shard_map/ppermute | solution.py:22
  83.5 1.2 collective-permute-done.8
  84.9 2.5 %collective-permute-start.11 = (f32[2,1,46,7]{3,2,1,0:T(8,128)S(1)}, f32[2,1,46,7]{3,2,1,0:T(8,128)S(1)}, u32[]{:S(2)}, u32[]{:S(2)}) collective-permute-start(f32[2,1,46,7]{3,2,1,0:T(8,128)S(1)} %get-tuple-element.49), channel_id=1, source_target_pairs={{1,0},{2,1},{3,2},{0,3},{5,4},{6,5},{7,6},{4,7},{9,8},{10,9},{11,1... | collective-permute-start | bytes 7736 | tf_op jit(solution)/shard_map/ppermute | solution.py:22
  88.1 5.1 %stack.171 = f32[8,1]{0,1:T(1,128)S(1)} concatenate(f32[1,1]{0,1:T(1,128)} %bitcast.35, f32[1,1]{0,1:T(1,128)} %bitcast.36, f32[1,1]{0,1:T(1,128)} %bitcast.37, f32[1,1]{0,1:T(1,128)} %bitcast.38, f32[1,1]{0,1:T(1,128)} %bitcast.39, f32[1,1]{0,1:T(1,128)} %bitcast.40, f32[1,1]{0,1:T(1,128)} %bitcast.41, f32[1,1]{0,1:T(1,128)} %bitcast.42), dimensions={0} | concatenate | bytes 64 | tf_op jit(solution)/shard_map/stack | solution.py:116
  93.9 1.1 concatenate.135
  95.5 0.8 fusion.62
  97.0 0.8 fusion.61
  99.8 0.8 multiply_reduce_fusion.3
  103.6 1.0 multiply_reduce_fusion
  105.1 5.2 %stack.181 = f32[8,1]{0,1:T(1,128)S(1)} concatenate(f32[1,1]{0,1:T(1,128)} %bitcast.44, f32[1,1]{0,1:T(1,128)} %bitcast.45, f32[1,1]{0,1:T(1,128)} %bitcast.46, f32[1,1]{0,1:T(1,128)} %bitcast.47, f32[1,1]{0,1:T(1,128)} %bitcast.48, f32[1,1]{0,1:T(1,128)} %bitcast.49, f32[1,1]{0,1:T(1,128)} %bitcast.50, f32[1,1]{0,1:T(1,128)} %bitcast.51), dimensions={0} | concatenate | bytes 64 | tf_op jit(solution)/shard_map/stack | solution.py:116
  110.3 0.8 multiply_reduce_fusion.10
  111.1 40.4 %all-reduce = (f32[1]{0:T(128)}, f32[8,1]{0,1:T(1,128)S(1)}, f32[8,1]{0,1:T(1,128)S(1)}) all-reduce(f32[1]{0:T(128)} %bitcast.31, f32[8,1]{0,1:T(1,128)S(1)} %stack.181, f32[8,1]{0,1:T(1,128)S(1)} %stack.171), channel_id=1, replica_groups=mesh['gx'=8,'gy'=4] {'gx','gy'}, use_global_device_ids=true, to_apply=%region_5.6 | all-reduce | flops 17 | bytes 136 | tf_op jit(solution)/shard_map/psum | solution.py:118
  (195 shorter events, 24.9 us)
Async XLA Ops:
  0.6 8.4 %copy-start.54 = (f32[16]{0:T(128)S(1)}, f32[16]{0:T(128)}, u32[]{:S(2)}) copy-start(f32[16]{0:T(128)} %param.13) | copy-start | bytes 196
  0.6 8.4 %copy-start.52 = (s32[32,1024]{1,0:T(8,128)S(1)}, s32[32,1024]{1,0:T(8,128)}, u32[]{:S(2)}) copy-start(s32[32,1024]{1,0:T(8,128)} %param.12) | copy-start | bytes 393220
  0.7 8.4 %copy-start.51 = (s32[32,1024]{1,0:T(8,128)S(1)}, s32[32,1024]{1,0:T(8,128)}, u32[]{:S(2)}) copy-start(s32[32,1024]{1,0:T(8,128)} %param.11) | copy-start | bytes 393220
  3.3 6.3 %copy-start.50 = (f32[32,1024]{1,0:T(8,128)S(1)}, f32[32,1024]{1,0:T(8,128)}, u32[]{:S(2)}) copy-start(f32[32,1024]{1,0:T(8,128)} %param.10) | copy-start | bytes 393220
  4.4 10.8 %collective-permute-start.4 = (f32[2,1,7,1024]{3,2,1,0:T(8,128)S(1)}, f32[2,1,7,1024]{3,2,1,0:T(8,128)S(1)}, u32[]{:S(2)}, u32[]{:S(2)}) collective-permute-start(f32[2,1,7,1024]{3,2,1,0:T(8,128)S(1)} %get-tuple-element.79), channel_id=1, source_target_pairs={{0,4},{4,8},{8,12},{12,16},{16,20},{20,24},{24,28},{28,0},{1,5},{5... | collective-permute-start | bytes 172040 | tf_op jit(solution)/shard_map/ppermute | solution.py:19
  5.0 10.3 %collective-permute-start.5 = (f32[2,1,7,1024]{3,2,1,0:T(8,128)S(1)}, f32[2,1,7,1024]{3,2,1,0:T(8,128)S(1)}, u32[]{:S(2)}, u32[]{:S(2)}) collective-permute-start(f32[2,1,7,1024]{3,2,1,0:T(8,128)S(1)} %get-tuple-element.80), channel_id=1, source_target_pairs={{4,0},{8,4},{12,8},{16,12},{20,16},{24,20},{28,24},{0,28},{5,1},{9... | collective-permute-start | bytes 172040 | tf_op jit(solution)/shard_map/ppermute | solution.py:22
  9.6 6.2 %collective-permute-start = (f32[3,7,1024]{2,1,0:T(8,128)S(1)}, f32[3,7,1024]{2,1,0:T(8,128)S(1)}, u32[]{:S(2)}, u32[]{:S(2)}) collective-permute-start(f32[3,7,1024]{2,1,0:T(8,128)S(1)} %get-tuple-element.51), channel_id=1, source_target_pairs={{0,4},{4,8},{8,12},{12,16},{16,20},{20,24},{24,28},{28,0},{1,5},{5... | collective-permute-start | bytes 258056 | tf_op jit(solution)/shard_map/ppermute | solution.py:19
  9.7 6.1 %collective-permute-start.1 = (f32[3,7,1024]{2,1,0:T(8,128)S(1)}, f32[3,7,1024]{2,1,0:T(8,128)S(1)}, u32[]{:S(2)}, u32[]{:S(2)}) collective-permute-start(f32[3,7,1024]{2,1,0:T(8,128)S(1)} %get-tuple-element.52), channel_id=1, source_target_pairs={{4,0},{8,4},{12,8},{16,12},{20,16},{24,20},{28,24},{0,28},{5,1},{9... | collective-permute-start | bytes 258056 | tf_op jit(solution)/shard_map/ppermute | solution.py:22
  16.0 11.6 %collective-permute-start.3 = (f32[3,46,7]{2,1,0:T(8,128)S(1)}, f32[3,46,7]{2,1,0:T(8,128)S(1)}, u32[]{:S(2)}, u32[]{:S(2)}) collective-permute-start(f32[3,46,7]{2,1,0:T(8,128)S(1)} %get-tuple-element.39), channel_id=1, source_target_pairs={{1,0},{2,1},{3,2},{0,3},{5,4},{6,5},{7,6},{4,7},{9,8},{10,9},{11,1... | collective-permute-start | bytes 11600 | tf_op jit(solution)/shard_map/ppermute | solution.py:22
  19.3 8.2 %collective-permute-start.2 = (f32[3,46,7]{2,1,0:T(8,128)S(1)}, f32[3,46,7]{2,1,0:T(8,128)S(1)}, u32[]{:S(2)}, u32[]{:S(2)}) collective-permute-start(f32[3,46,7]{2,1,0:T(8,128)S(1)} %get-tuple-element.40), channel_id=1, source_target_pairs={{0,1},{1,2},{2,3},{3,0},{4,5},{5,6},{6,7},{7,4},{8,9},{9,10},{10,1... | collective-permute-start | bytes 11600 | tf_op jit(solution)/shard_map/ppermute | solution.py:19
  19.4 4.7 %collective-permute-start.7 = (f32[2,1,46,7]{3,2,1,0:T(8,128)S(1)}, f32[2,1,46,7]{3,2,1,0:T(8,128)S(1)}, u32[]{:S(2)}, u32[]{:S(2)}) collective-permute-start(f32[2,1,46,7]{3,2,1,0:T(8,128)S(1)} %get-tuple-element.53), channel_id=1, source_target_pairs={{1,0},{2,1},{3,2},{0,3},{5,4},{6,5},{7,6},{4,7},{9,8},{10,9},{11,1... | collective-permute-start | bytes 7736 | tf_op jit(solution)/shard_map/ppermute | solution.py:22
  22.4 5.0 %collective-permute-start.6 = (f32[2,1,46,7]{3,2,1,0:T(8,128)S(1)}, f32[2,1,46,7]{3,2,1,0:T(8,128)S(1)}, u32[]{:S(2)}, u32[]{:S(2)}) collective-permute-start(f32[2,1,46,7]{3,2,1,0:T(8,128)S(1)} %get-tuple-element.54), channel_id=1, source_target_pairs={{0,1},{1,2},{2,3},{3,0},{4,5},{5,6},{6,7},{7,4},{8,9},{9,10},{10,1... | collective-permute-start | bytes 7736 | tf_op jit(solution)/shard_map/ppermute | solution.py:19
  33.3 4.3 %copy-start.2 = (f32[34,1026]{1,0:T(8,128)}, f32[34,1026]{1,0:T(8,128)S(1)}, u32[]{:S(2)}) copy-start(f32[34,1026]{1,0:T(8,128)S(1)} %slice.944) | copy-start | bytes 418612
  33.4 2.3 %copy-start.6 = (f32[38,1030]{1,0:T(8,128)}, f32[38,1030]{1,0:T(8,128)S(1)}, u32[]{:S(2)}) copy-start(f32[38,1030]{1,0:T(8,128)S(1)} %slice.914) | copy-start | bytes 469684
  33.6 3.0 %copy-start.4 = (f32[36,1028]{1,0:T(8,128)}, f32[36,1028]{1,0:T(8,128)S(1)}, u32[]{:S(2)}) copy-start(f32[36,1028]{1,0:T(8,128)S(1)} %slice.928) | copy-start | bytes 444100
  79.2 5.5 %collective-permute-start.8 = (f32[2,1,7,1024]{3,2,1,0:T(8,128)S(1)}, f32[2,1,7,1024]{3,2,1,0:T(8,128)S(1)}, u32[]{:S(2)}, u32[]{:S(2)}) collective-permute-start(f32[2,1,7,1024]{3,2,1,0:T(8,128)S(1)} %get-tuple-element.75), channel_id=1, source_target_pairs={{0,4},{4,8},{8,12},{12,16},{16,20},{20,24},{24,28},{28,0},{1,5},{5... | collective-permute-start | bytes 172040 | tf_op jit(solution)/shard_map/ppermute | solution.py:19
  79.3 5.5 %collective-permute-start.9 = (f32[2,1,7,1024]{3,2,1,0:T(8,128)S(1)}, f32[2,1,7,1024]{3,2,1,0:T(8,128)S(1)}, u32[]{:S(2)}, u32[]{:S(2)}) collective-permute-start(f32[2,1,7,1024]{3,2,1,0:T(8,128)S(1)} %get-tuple-element.76), channel_id=1, source_target_pairs={{4,0},{8,4},{12,8},{16,12},{20,16},{24,20},{28,24},{0,28},{5,1},{9... | collective-permute-start | bytes 172040 | tf_op jit(solution)/shard_map/ppermute | solution.py:22
  84.9 8.4 %collective-permute-start.11 = (f32[2,1,46,7]{3,2,1,0:T(8,128)S(1)}, f32[2,1,46,7]{3,2,1,0:T(8,128)S(1)}, u32[]{:S(2)}, u32[]{:S(2)}) collective-permute-start(f32[2,1,46,7]{3,2,1,0:T(8,128)S(1)} %get-tuple-element.49), channel_id=1, source_target_pairs={{1,0},{2,1},{3,2},{0,3},{5,4},{6,5},{7,6},{4,7},{9,8},{10,9},{11,1... | collective-permute-start | bytes 7736 | tf_op jit(solution)/shard_map/ppermute | solution.py:22
  87.4 6.5 %collective-permute-start.10 = (f32[2,1,46,7]{3,2,1,0:T(8,128)S(1)}, f32[2,1,46,7]{3,2,1,0:T(8,128)}, u32[]{:S(2)}, u32[]{:S(2)}) collective-permute-start(f32[2,1,46,7]{3,2,1,0:T(8,128)S(1)} %get-tuple-element.50), channel_id=1, source_target_pairs={{0,1},{1,2},{2,3},{3,0},{4,5},{5,6},{6,7},{7,4},{8,9},{9,10},{10,1... | collective-permute-start | bytes 7736 | tf_op jit(solution)/shard_map/ppermute | solution.py:19
  96.3 1.5 copy-start.9
  96.3 1.5 copy-start.11
  96.3 1.5 copy-start.13
  96.3 1.5 copy-start.15
  96.4 1.5 copy-start.17
  (43 other events, 45.9 us)
where the time goes:
time: 154 us
  blocking collectives  77.4 us (50%)
  other arithmetic  23.4 us (15%)
  local copies, waits for them, and re-layouts  21.2 us (14%)
  starting transfers between devices  20.6 us (13%)
  waiting for transfers between devices  6.73 us (4%)
  between operations  4.29 us (3%)
    psum x2, blocking collectives, per_device(): term_total, state_total = lax.psum((term_local, state_local), ('gx', 'gy'))  77.4 us
    ppermute x6, starting transfers between devices, padded(): lax.ppermute(lax.slice_in_dim(block, 0, width, axis=dim), axis, backward)  19.9 us
    another operation x2, local copies, waits for them, and re-layouts, per_device(): jnp.stack([jnp.sum(vector * vector, axis=(0, 2, 3)) for vector in chebysh...  10.4 us
    reduce_sum x12, other arithmetic, per_device(): jnp.sum(vector * vector, axis=(0, 2, 3))  9.75 us
    sub x10, other arithmetic, per_device(): following = 2.0 * applied - shrink(previous, previous_margin - margin + 1)  5.76 us
    ppermute x6, waiting for transfers between devices, padded(): lax.ppermute(lax.slice_in_dim(block, block.shape[dim] - width, None, axis...  4.9 us
    unnamed x110, local copies, waits for them, and re-layouts  3.2 us
  transfers between devices with their start and end apart: 12, of which 4 were waited for; matrix products, arithmetic and copies ran while one was open for 5% of the time, Pallas kernels for 0%

commit v1 on v0

--- a/solution.py
+++ b/solution.py
@@ -1,3 +1,4 @@
+import functools
 import math
 import jax
 import jax.numpy as jnp
@@ -8,6 +9,14 @@
 STEPS = 2
 SPECTRAL = 7.5
 epsilon = 1e-06
+
+
+def trace_the_sources_all(inp, device_axis, mesh_name):
+    mixed_arr = lax.psum(inp, device_axis)
+    return lax.psum(mixed_arr, mesh_name)
+
+
+copies_meet = functools.partial(trace_the_sources_all, device_axis="gy", mesh_name="gx")
 
 
 def padded(block, sides, width):
@@ -115,7 +124,7 @@
             accumulate = accumulate + weights[degree] * jnp.stack([real_rot, imag_rot])
         term_local = jnp.stack([jnp.sum(vector * vector, axis=(0, 2, 3)) for vector in chebyshev])
         state_local = jnp.sum(accumulate * accumulate, axis=(0, 2, 3))
-        term_total, state_total = lax.psum((term_local, state_local), ("gx", "gy"))
+        term_total, state_total = copies_meet((term_local, state_local))
         norm_rows.append(term_total / cell_count)
         rescale = lax.rsqrt(state_total / cell_count + epsilon)
         packet_state = accumulate * rescale[None, :, None, None]

time: 154 us -> 123 us (0.80)
  blocking collectives: 77.4 us -> 48.3 us
  local copies, waits for them, and re-layouts: 21.2 us -> 19.6 us
    psum x2 -> x4, blocking collectives: 77.4 us -> 48.3 us  [the longest x2 29.4 us: trace_the_sources_all(): return lax.psum(mixed_arr, mesh_name)]
    unnamed x110 -> x116, local copies, waits for them, and re-layouts: 3.2 us -> 2.61 us
  transfers between devices with their start and end apart: 12 -> 12, of which waited for: 4 -> 4; matrix products, arithmetic and copies ran while one was open for 5% -> 7% of each run, Pallas kernels for 0% -> 0%
where the time goes in v1:
time: 123 us; the launch traced here: 122 us
  blocking collectives  48.3 us (39%)
  other arithmetic  23.2 us (19%)
  starting transfers between devices  20.3 us (17%)
  local copies, waits for them, and re-layouts  19.6 us (16%)
  waiting for transfers between devices  6.77 us (6%)
  between operations  4.27 us (3%)
    psum x2, blocking collectives, trace_the_sources_all(): return lax.psum(mixed_arr, mesh_name)  29.4 us
    ppermute x6, starting transfers between devices, padded(): lax.ppermute(lax.slice_in_dim(block, 0, width, axis=dim), axis, backward)  19.5 us
    psum x2, blocking collectives, trace_the_sources_all(): mixed_arr = lax.psum(inp, device_axis)  18.9 us
    another operation x2, local copies, waits for them, and re-layouts, per_device(): jnp.stack([jnp.sum(vector * vector, axis=(0, 2, 3)) for vector in chebysh...  10.2 us
    reduce_sum x12, other arithmetic, per_device(): jnp.sum(vector * vector, axis=(0, 2, 3))  9.57 us
    sub x10, other arithmetic, per_device(): following = 2.0 * applied - shrink(previous, previous_margin - margin + 1)  5.79 us
    ppermute x6, waiting for transfers between devices, padded(): lax.ppermute(lax.slice_in_dim(block, block.shape[dim] - width, None, axis...  4.94 us
    unnamed x116, local copies, waits for them, and re-layouts  2.61 us
  transfers between devices with their start and end apart: 12, of which 4 were waited for; matrix products, arithmetic and copies ran while one was open for 7% of the time, Pallas kernels for 0%

profile of v1, /device:TPU:0, one launch (start us, length us, event | category | flops | bytes accessed | tf_op | source)
XLA Modules:
  0.0 122.5 jit_solution(7601375204090458591)
XLA Ops:
  0.7 1.3 %fusion.128 = (s32[1,1]{1,0:T(1,128)}, s32[1,1]{1,0:T(1,128)}) fusion(s32[1,2]{1,0:T(1,128)} %param.14), kind=kLoop, calls=%fused_computation.302 | loop fusion | bytes 16 | tf_op jit(solution)/shard_map/slice | solution.py:98
  3.3 1.1 multiply_bitcast_fusion
  5.0 4.1 %collective-permute-start.5 = (f32[2,1,7,1024]{3,2,1,0:T(8,128)S(1)}, f32[2,1,7,1024]{3,2,1,0:T(8,128)S(1)}, u32[]{:S(2)}, u32[]{:S(2)}) collective-permute-start(f32[2,1,7,1024]{3,2,1,0:T(8,128)S(1)} %get-tuple-element.83), channel_id=1, source_target_pairs={{4,0},{8,4},{12,8},{16,12},{20,16},{24,20},{28,24},{0,28},{5,1},{9... | collective-permute-start | bytes 172040 | tf_op jit(solution)/shard_map/ppermute | solution.py:31
  9.7 3.5 %collective-permute-start.1 = (f32[3,7,1024]{2,1,0:T(8,128)S(1)}, f32[3,7,1024]{2,1,0:T(8,128)S(1)}, u32[]{:S(2)}, u32[]{:S(2)}) collective-permute-start(f32[3,7,1024]{2,1,0:T(8,128)S(1)} %get-tuple-element.55), channel_id=1, source_target_pairs={{4,0},{8,4},{12,8},{16,12},{20,16},{24,20},{28,24},{0,28},{5,1},{9... | collective-permute-start | bytes 258056 | tf_op jit(solution)/shard_map/ppermute | solution.py:31
  16.0 3.4 %collective-permute-start.3 = (f32[3,46,7]{2,1,0:T(8,128)S(1)}, f32[3,46,7]{2,1,0:T(8,128)S(1)}, u32[]{:S(2)}, u32[]{:S(2)}) collective-permute-start(f32[3,46,7]{2,1,0:T(8,128)S(1)} %get-tuple-element.42), channel_id=1, source_target_pairs={{1,0},{2,1},{3,2},{0,3},{5,4},{6,5},{7,6},{4,7},{9,8},{10,9},{11,1... | collective-permute-start | bytes 11600 | tf_op jit(solution)/shard_map/ppermute | solution.py:31
  19.4 2.9 %collective-permute-start.7 = (f32[2,1,46,7]{3,2,1,0:T(8,128)S(1)}, f32[2,1,46,7]{3,2,1,0:T(8,128)S(1)}, u32[]{:S(2)}, u32[]{:S(2)}) collective-permute-start(f32[2,1,46,7]{3,2,1,0:T(8,128)S(1)} %get-tuple-element.56), channel_id=1, source_target_pairs={{1,0},{2,1},{3,2},{0,3},{5,4},{6,5},{7,6},{4,7},{9,8},{10,9},{11,1... | collective-permute-start | bytes 7736 | tf_op jit(solution)/shard_map/ppermute | solution.py:31
  22.4 1.8 %collective-permute-done.7 = f32[2,1,46,7]{3,2,1,0:T(8,128)S(1)} collective-permute-done((f32[2,1,46,7]{3,2,1,0:T(8,128)S(1)}, f32[2,1,46,7]{3,2,1,0:T(8,128)S(1)}, u32[]{:S(2)}, u32[]{:S(2)}) %collective-permute-start.7) | collective-permute-done | bytes 2608 | tf_op jit(solution)/shard_map/ppermute | solution.py:31
  24.2 3.2 %collective-permute-done.6 = f32[2,1,46,7]{3,2,1,0:T(8,128)S(1)} collective-permute-done((f32[2,1,46,7]{3,2,1,0:T(8,128)S(1)}, f32[2,1,46,7]{3,2,1,0:T(8,128)S(1)}, u32[]{:S(2)}, u32[]{:S(2)}) %collective-permute-start.6) | collective-permute-done | bytes 2608 | tf_op jit(solution)/shard_map/ppermute | solution.py:28
  30.3 0.8 fusion.65
  38.0 1.1 multiply_reduce_fusion.5
  39.2 0.9 multiply_reduce_fusion.11
  40.0 8.1 %psum.56 = f32[1]{0:T(128)} all-reduce(f32[1]{0:T(128)} %bitcast.29), channel_id=1, replica_groups=mesh['gx'=8,'gy'=4] {'gy'}, use_global_device_ids=true, to_apply=%region_3.4 | all-reduce | flops 1 | bytes 8 | tf_op jit(solution)/shard_map/psum | solution.py:15
  48.8 14.2 %psum.57 = f32[1]{0:T(128)} all-reduce(f32[1]{0:T(128)} %psum.56), channel_id=1, replica_groups=mesh['gx'=8,'gy'=4] {'gx'}, use_global_device_ids=true, to_apply=%region_4.5 | all-reduce | flops 1 | bytes 8 | tf_op jit(solution)/shard_map/psum | solution.py:16
  64.5 3.5 %collective-permute-start.9 = (f32[2,1,7,1024]{3,2,1,0:T(8,128)S(1)}, f32[2,1,7,1024]{3,2,1,0:T(8,128)S(1)}, u32[]{:S(2)}, u32[]{:S(2)}) collective-permute-start(f32[2,1,7,1024]{3,2,1,0:T(8,128)S(1)} %get-tuple-element.79), channel_id=1, source_target_pairs={{4,0},{8,4},{12,8},{16,12},{20,16},{24,20},{28,24},{0,28},{5,1},{9... | collective-permute-start | bytes 172040 | tf_op jit(solution)/shard_map/ppermute | solution.py:31
  68.0 0.8 fusion.63
  68.8 1.2 collective-permute-done.8
  70.1 2.0 %collective-permute-start.11 = (f32[2,1,46,7]{3,2,1,0:T(8,128)S(1)}, f32[2,1,46,7]{3,2,1,0:T(8,128)S(1)}, u32[]{:S(2)}, u32[]{:S(2)}) collective-permute-start(f32[2,1,46,7]{3,2,1,0:T(8,128)S(1)} %get-tuple-element.52), channel_id=1, source_target_pairs={{1,0},{2,1},{3,2},{0,3},{5,4},{6,5},{7,6},{4,7},{9,8},{10,9},{11,1... | collective-permute-start | bytes 7736 | tf_op jit(solution)/shard_map/ppermute | solution.py:31
  73.1 5.1 %stack.171 = f32[8,1]{0,1:T(1,128)S(1)} concatenate(f32[1,1]{0,1:T(1,128)} %bitcast.35, f32[1,1]{0,1:T(1,128)} %bitcast.36, f32[1,1]{0,1:T(1,128)} %bitcast.37, f32[1,1]{0,1:T(1,128)} %bitcast.38, f32[1,1]{0,1:T(1,128)} %bitcast.39, f32[1,1]{0,1:T(1,128)} %bitcast.40, f32[1,1]{0,1:T(1,128)} %bitcast.41, f32[1,1]{0,1:T(1,128)} %bitcast.42), dimensions={0} | concatenate | bytes 64 | tf_op jit(solution)/shard_map/stack | solution.py:125
  80.4 0.8 fusion.61
  87.0 1.0 multiply_reduce_fusion
  88.5 5.2 %stack.181 = f32[8,1]{0,1:T(1,128)S(1)} concatenate(f32[1,1]{0,1:T(1,128)} %bitcast.44, f32[1,1]{0,1:T(1,128)} %bitcast.45, f32[1,1]{0,1:T(1,128)} %bitcast.46, f32[1,1]{0,1:T(1,128)} %bitcast.47, f32[1,1]{0,1:T(1,128)} %bitcast.48, f32[1,1]{0,1:T(1,128)} %bitcast.49, f32[1,1]{0,1:T(1,128)} %bitcast.50, f32[1,1]{0,1:T(1,128)} %bitcast.51), dimensions={0} | concatenate | bytes 64 | tf_op jit(solution)/shard_map/stack | solution.py:125
  93.6 0.8 multiply_reduce_fusion.10
  94.5 10.8 %all-reduce.1 = (f32[1]{0:T(128)}, f32[8,1]{0,1:T(1,128)S(1)}, f32[8,1]{0,1:T(1,128)S(1)}) all-reduce(f32[1]{0:T(128)} %bitcast.31, f32[8,1]{0,1:T(1,128)S(1)} %stack.181, f32[8,1]{0,1:T(1,128)S(1)} %stack.171), channel_id=1, replica_groups=mesh['gx'=8,'gy'=4] {'gy'}, use_global_device_ids=true, to_apply=%region_6.7 | all-reduce | flops 17 | bytes 136 | tf_op jit(solution)/shard_map/psum | solution.py:15
  105.3 15.2 %all-reduce = (f32[1]{0:T(128)}, f32[8,1]{0,1:T(1,128)S(1)}, f32[8,1]{0,1:T(1,128)S(1)}) all-reduce(f32[1]{0:T(128)} %get-tuple-element.8, f32[8,1]{0,1:T(1,128)S(1)} %get-tuple-element.9, f32[8,1]{0,1:T(1,128)S(1)} %get-tuple-element.10), channel_id=1, replica_groups=mesh['gx'=8,'gy'=4] {'gx'}, use_global_device_ids=true, to_apply=%region_7.8 | all-reduce | flops 17 | bytes 136 | tf_op jit(solution)/shard_map/psum | solution.py:16
  (203 shorter events, 25.5 us)
Async XLA Ops:
  0.6 8.4 %copy-start.57 = (f32[16]{0:T(128)S(1)}, f32[16]{0:T(128)}, u32[]{:S(2)}) copy-start(f32[16]{0:T(128)} %param.13) | copy-start | bytes 196
  0.6 8.4 %copy-start.56 = (s32[32,1024]{1,0:T(8,128)S(1)}, s32[32,1024]{1,0:T(8,128)}, u32[]{:S(2)}) copy-start(s32[32,1024]{1,0:T(8,128)} %param.12) | copy-start | bytes 393220
  0.7 8.4 %copy-start.55 = (s32[32,1024]{1,0:T(8,128)S(1)}, s32[32,1024]{1,0:T(8,128)}, u32[]{:S(2)}) copy-start(s32[32,1024]{1,0:T(8,128)} %param.11) | copy-start | bytes 393220
  3.3 6.3 %copy-start.54 = (f32[32,1024]{1,0:T(8,128)S(1)}, f32[32,1024]{1,0:T(8,128)}, u32[]{:S(2)}) copy-start(f32[32,1024]{1,0:T(8,128)} %param.10) | copy-start | bytes 393220
  4.4 10.7 %collective-permute-start.4 = (f32[2,1,7,1024]{3,2,1,0:T(8,128)S(1)}, f32[2,1,7,1024]{3,2,1,0:T(8,128)S(1)}, u32[]{:S(2)}, u32[]{:S(2)}) collective-permute-start(f32[2,1,7,1024]{3,2,1,0:T(8,128)S(1)} %get-tuple-element.82), channel_id=1, source_target_pairs={{0,4},{4,8},{8,12},{12,16},{16,20},{20,24},{24,28},{28,0},{1,5},{5... | collective-permute-start | bytes 172040 | tf_op jit(solution)/shard_map/ppermute | solution.py:28
  5.0 10.2 %collective-permute-start.5 = (f32[2,1,7,1024]{3,2,1,0:T(8,128)S(1)}, f32[2,1,7,1024]{3,2,1,0:T(8,128)S(1)}, u32[]{:S(2)}, u32[]{:S(2)}) collective-permute-start(f32[2,1,7,1024]{3,2,1,0:T(8,128)S(1)} %get-tuple-element.83), channel_id=1, source_target_pairs={{4,0},{8,4},{12,8},{16,12},{20,16},{24,20},{28,24},{0,28},{5,1},{9... | collective-permute-start | bytes 172040 | tf_op jit(solution)/shard_map/ppermute | solution.py:31
  9.6 6.2 %collective-permute-start = (f32[3,7,1024]{2,1,0:T(8,128)S(1)}, f32[3,7,1024]{2,1,0:T(8,128)S(1)}, u32[]{:S(2)}, u32[]{:S(2)}) collective-permute-start(f32[3,7,1024]{2,1,0:T(8,128)S(1)} %get-tuple-element.54), channel_id=1, source_target_pairs={{0,4},{4,8},{8,12},{12,16},{16,20},{20,24},{24,28},{28,0},{1,5},{5... | collective-permute-start | bytes 258056 | tf_op jit(solution)/shard_map/ppermute | solution.py:28
  9.7 6.1 %collective-permute-start.1 = (f32[3,7,1024]{2,1,0:T(8,128)S(1)}, f32[3,7,1024]{2,1,0:T(8,128)S(1)}, u32[]{:S(2)}, u32[]{:S(2)}) collective-permute-start(f32[3,7,1024]{2,1,0:T(8,128)S(1)} %get-tuple-element.55), channel_id=1, source_target_pairs={{4,0},{8,4},{12,8},{16,12},{20,16},{24,20},{28,24},{0,28},{5,1},{9... | collective-permute-start | bytes 258056 | tf_op jit(solution)/shard_map/ppermute | solution.py:31
  16.0 11.6 %collective-permute-start.3 = (f32[3,46,7]{2,1,0:T(8,128)S(1)}, f32[3,46,7]{2,1,0:T(8,128)S(1)}, u32[]{:S(2)}, u32[]{:S(2)}) collective-permute-start(f32[3,46,7]{2,1,0:T(8,128)S(1)} %get-tuple-element.42), channel_id=1, source_target_pairs={{1,0},{2,1},{3,2},{0,3},{5,4},{6,5},{7,6},{4,7},{9,8},{10,9},{11,1... | collective-permute-start | bytes 11600 | tf_op jit(solution)/shard_map/ppermute | solution.py:31
  19.3 8.3 %collective-permute-start.2 = (f32[3,46,7]{2,1,0:T(8,128)S(1)}, f32[3,46,7]{2,1,0:T(8,128)S(1)}, u32[]{:S(2)}, u32[]{:S(2)}) collective-permute-start(f32[3,46,7]{2,1,0:T(8,128)S(1)} %get-tuple-element.43), channel_id=1, source_target_pairs={{0,1},{1,2},{2,3},{3,0},{4,5},{5,6},{6,7},{7,4},{8,9},{9,10},{10,1... | collective-permute-start | bytes 11600 | tf_op jit(solution)/shard_map/ppermute | solution.py:28
  19.4 4.7 %collective-permute-start.7 = (f32[2,1,46,7]{3,2,1,0:T(8,128)S(1)}, f32[2,1,46,7]{3,2,1,0:T(8,128)S(1)}, u32[]{:S(2)}, u32[]{:S(2)}) collective-permute-start(f32[2,1,46,7]{3,2,1,0:T(8,128)S(1)} %get-tuple-element.56), channel_id=1, source_target_pairs={{1,0},{2,1},{3,2},{0,3},{5,4},{6,5},{7,6},{4,7},{9,8},{10,9},{11,1... | collective-permute-start | bytes 7736 | tf_op jit(solution)/shard_map/ppermute | solution.py:31
  22.4 5.0 %collective-permute-start.6 = (f32[2,1,46,7]{3,2,1,0:T(8,128)S(1)}, f32[2,1,46,7]{3,2,1,0:T(8,128)S(1)}, u32[]{:S(2)}, u32[]{:S(2)}) collective-permute-start(f32[2,1,46,7]{3,2,1,0:T(8,128)S(1)} %get-tuple-element.57), channel_id=1, source_target_pairs={{0,1},{1,2},{2,3},{3,0},{4,5},{5,6},{6,7},{7,4},{8,9},{9,10},{10,1... | collective-permute-start | bytes 7736 | tf_op jit(solution)/shard_map/ppermute | solution.py:28
  31.4 5.4 %copy-start.6 = (f32[34,1026]{1,0:T(8,128)}, f32[34,1026]{1,0:T(8,128)S(1)}, u32[]{:S(2)}) copy-start(f32[34,1026]{1,0:T(8,128)S(1)} %slice.944) | copy-start | bytes 418612
  31.5 3.4 %copy-start.10 = (f32[38,1030]{1,0:T(8,128)}, f32[38,1030]{1,0:T(8,128)S(1)}, u32[]{:S(2)}) copy-start(f32[38,1030]{1,0:T(8,128)S(1)} %slice.914) | copy-start | bytes 469684
  31.6 4.1 %copy-start.8 = (f32[36,1028]{1,0:T(8,128)}, f32[36,1028]{1,0:T(8,128)S(1)}, u32[]{:S(2)}) copy-start(f32[36,1028]{1,0:T(8,128)S(1)} %slice.928) | copy-start | bytes 444100
  31.8 6.3 %copy-start.44 = (f32[32,1024]{1,0:T(8,128)}, f32[32,1024]{1,0:T(8,128)S(1)}, u32[]{:S(2)}) copy-start(f32[32,1024]{1,0:T(8,128)S(1)} %slice.960) | copy-start | bytes 393220
  31.9 1.6 %copy-start.12 = (f32[40,1032]{1,0:T(8,128)}, f32[40,1032]{1,0:T(8,128)S(1)}, u32[]{:S(2)}) copy-start(f32[40,1032]{1,0:T(8,128)S(1)} %slice.898) | copy-start | bytes 495364
  64.4 5.5 %collective-permute-start.8 = (f32[2,1,7,1024]{3,2,1,0:T(8,128)S(1)}, f32[2,1,7,1024]{3,2,1,0:T(8,128)S(1)}, u32[]{:S(2)}, u32[]{:S(2)}) collective-permute-start(f32[2,1,7,1024]{3,2,1,0:T(8,128)S(1)} %get-tuple-element.78), channel_id=1, source_target_pairs={{0,4},{4,8},{8,12},{12,16},{16,20},{20,24},{24,28},{28,0},{1,5},{5... | collective-permute-start | bytes 172040 | tf_op jit(solution)/shard_map/ppermute | solution.py:28
  64.5 5.5 %collective-permute-start.9 = (f32[2,1,7,1024]{3,2,1,0:T(8,128)S(1)}, f32[2,1,7,1024]{3,2,1,0:T(8,128)S(1)}, u32[]{:S(2)}, u32[]{:S(2)}) collective-permute-start(f32[2,1,7,1024]{3,2,1,0:T(8,128)S(1)} %get-tuple-element.79), channel_id=1, source_target_pairs={{4,0},{8,4},{12,8},{16,12},{20,16},{24,20},{28,24},{0,28},{5,1},{9... | collective-permute-start | bytes 172040 | tf_op jit(solution)/shard_map/ppermute | solution.py:31
  70.1 8.0 %collective-permute-start.11 = (f32[2,1,46,7]{3,2,1,0:T(8,128)S(1)}, f32[2,1,46,7]{3,2,1,0:T(8,128)S(1)}, u32[]{:S(2)}, u32[]{:S(2)}) collective-permute-start(f32[2,1,46,7]{3,2,1,0:T(8,128)S(1)} %get-tuple-element.52), channel_id=1, source_target_pairs={{1,0},{2,1},{3,2},{0,3},{5,4},{6,5},{7,6},{4,7},{9,8},{10,9},{11,1... | collective-permute-start | bytes 7736 | tf_op jit(solution)/shard_map/ppermute | solution.py:31
  72.1 6.0 %collective-permute-start.10 = (f32[2,1,46,7]{3,2,1,0:T(8,128)S(1)}, f32[2,1,46,7]{3,2,1,0:T(8,128)S(1)}, u32[]{:S(2)}, u32[]{:S(2)}) collective-permute-start(f32[2,1,46,7]{3,2,1,0:T(8,128)S(1)} %get-tuple-element.53), channel_id=1, source_target_pairs={{0,1},{1,2},{2,3},{3,0},{4,5},{5,6},{6,7},{7,4},{8,9},{9,10},{10,1... | collective-permute-start | bytes 7736 | tf_op jit(solution)/shard_map/ppermute | solution.py:28
  79.7 1.5 %copy-start.13 = (f32[40,1032]{1,0:T(8,128)S(1)}, f32[40,1032]{1,0:T(8,128)}, u32[]{:S(2)}) copy-start(f32[40,1032]{1,0:T(8,128)} %copy-done.12) | copy-start | bytes 495364
  79.7 1.5 %copy-start.15 = (f32[40,1032]{1,0:T(8,128)S(1)}, f32[40,1032]{1,0:T(8,128)}, u32[]{:S(2)}) copy-start(f32[40,1032]{1,0:T(8,128)} %copy-done.14) | copy-start | bytes 495364
  79.7 1.5 %copy-start.17 = (f32[40,1032]{1,0:T(8,128)S(1)}, f32[40,1032]{1,0:T(8,128)}, u32[]{:S(2)}) copy-start(f32[40,1032]{1,0:T(8,128)} %copy-done.16) | copy-start | bytes 495364
  (46 other events, 49.4 us)
